TPU v7x, 32 devices: a whole 2x2x4 slice. The times are simulated.
32 devices in a mesh: branch: 4 (over y, x), attn: 8 (over z, core).
Axes of the slice: x: 2, y: 2, z: 4, core: 2. Of those that a mesh axis runs over, the one named last changes fastest.
Arguments:
- queries: bfloat16 [2, 32, 5120], P(None, ('branch', 'attn')), may hold values from -60 to 60
- new_kv: bfloat16 [2, 2, 32, 1024], P(None, None, ('branch', 'attn')), may hold values from -6 to 6
- tail_kv: bfloat16 [32, 63, 2, 1024], P(('branch', 'attn')), may hold values from -6 to 6
- pool_kv: bfloat16 [4, 288, 64, 2, 1024], P('branch', 'attn'), may hold values from -6 to 6
- resid: bfloat16 [2, 32, 5120], P(None, ('branch', 'attn')), may hold values from -0.3125 to 0.3125
- block_table: int32 [32, 144], P('branch'), may hold values from 0 to 287, as said below
- block_counts: int32 [32], P('branch'), may hold values from 36 to 144
- owner_map: int32 [4, 288], P('branch'), may hold values from 0 to 287, each once within a row
- fork_parent: int32 [4, 8], P('branch'), may hold values from 0 to 7, each once within a row
- norm_gain: bfloat16 [5120], replicated, may hold values from 0.5 to 1.5
- w_gate: bfloat16 [24576, 5120], P('attn', 'branch'), may hold values from -0.078125 to 0.078125
- w_up: bfloat16 [24576, 5120], P('attn', 'branch'), may hold values from -0.078125 to 0.078125
- w_down: bfloat16 [24576, 5120], P('attn', 'branch'), may hold values from -0.0390625 to 0.0390625
Outputs:
- layer_out: bfloat16 [2, 32, 5120], P(None, ('branch', 'attn'))
Inputs may be any that keep to these rules, and one draw needn't show every extreme that they name: `block_table`: each branch's list names 144 distinct logical blocks of its group; only the first block_counts entries are its ancestors.
All inputs are finite; a program needn't handle non-finite values.
Results may differ from a plain program's by a relative error of at most 0.015.
Values may be sent and summed in bfloat16 or wider, within the bound.
A program may use at most 128 MiB of HBM per device.

v0:
```python
import jax
import jax.numpy as jnp
from jax import lax
from jax.experimental import pallas as pl
from jax.experimental.pallas import tpu as pltpu
from jax.sharding import PartitionSpec as P

H = 40
KVH = 8
HD = 128
GRP = H // KVH
NEG = -1e30
EPS = 1e-06


def attend_kernel(q_ref, kv_ref, ex_ref, bias_ref, exbias_ref, acc_ref, m_ref, t_ref):
    q = q_ref[0]
    rows = bias_ref.shape[0]
    contract = (((1,), (1,)), ((), ()))

    def scored(keys, bias):
        s = lax.dot_general(q, keys, contract, preferred_element_type=jnp.float32)
        s = s.reshape(GRP, rows, s.shape[1]) * HD ** (-0.5) + bias[None]
        return s.reshape(GRP * rows, s.shape[2])

    s = scored(kv_ref[...], bias_ref[...])
    e = scored(ex_ref[...], exbias_ref[...])
    peak = jnp.maximum(
        jnp.max(s, axis=1, keepdims=True), jnp.max(e, axis=1, keepdims=True)
    )
    ps = jnp.exp(s - peak)
    pe = jnp.exp(e - peak)
    total = jnp.sum(ps, axis=1, keepdims=True) + jnp.sum(pe, axis=1, keepdims=True)
    ws = pltpu.roll(ps, 1, 1).astype(jnp.bfloat16)
    we = pltpu.roll(pe, 1, 1).astype(jnp.bfloat16)
    acc = jnp.dot(ws, kv_ref[...], preferred_element_type=jnp.float32)
    acc += jnp.dot(we, ex_ref[...], preferred_element_type=jnp.float32)
    acc_ref[0] = acc
    m_ref[0] = jnp.broadcast_to(peak, acc.shape)
    t_ref[0] = jnp.broadcast_to(total, acc.shape)


def attend(q, kv, ex, bias, exbias):
    n = q.shape[1]
    out = jax.ShapeDtypeStruct((KVH, n, HD), jnp.float32)
    head = pl.BlockSpec((1, n, HD), lambda h: (h, 0, 0))
    return pl.pallas_call(
        attend_kernel,
        grid=(KVH,),
        in_specs=[
            head,
            pl.BlockSpec((kv.shape[0], HD), lambda h: (0, h)),
            pl.BlockSpec((ex.shape[0], HD), lambda h: (0, h)),
            pl.BlockSpec(bias.shape, lambda h: (0, 0)),
            pl.BlockSpec(exbias.shape, lambda h: (0, 0)),
        ],
        out_specs=[head, head, head],
        out_shape=[out, out, out],
        compiler_params=pltpu.CompilerParams(vmem_limit_bytes=48 * 1024 * 1024),
    )(q, kv, ex, bias, exbias)


def partial_states(queries, new_kv, tail_kv, pool_kv, block_table, block_counts, owner_map, fork_parent):
    ranks = lax.axis_size("attn")
    mine = lax.axis_index("attn")
    nblk = pool_kv.shape[1]
    width = pool_kv.shape[2]
    kvd = pool_kv.shape[4]
    maxb = block_table.shape[1]
    pool_size = owner_map.shape[1]
    group_rows = 2 * ranks
    every_q = lax.all_gather(queries[:, 0], "attn", axis=0)
    q = (
        every_q.reshape(group_rows, KVH, GRP, HD)
        .transpose(1, 2, 0, 3)
        .reshape(KVH, GRP * group_rows, HD)
    )
    kv = pool_kv[0].reshape(nblk * width * 2, kvd)
    newest = jnp.concatenate([tail_kv[0], new_kv[0, :, 0][None]], axis=0)
    newest = newest.reshape(width * 2, kvd)
    second = jnp.pad(new_kv[1, :, 0], ((0, width * 2 - 2), (0, 0)))
    ex = jnp.concatenate([newest, second], axis=0)

    slots = mine * nblk + jnp.arange(nblk, dtype=jnp.int32)
    matches = owner_map[0][None, :] == slots[:, None]
    logical = jnp.sum(
        jnp.where(matches, jnp.arange(pool_size, dtype=jnp.int32)[None, :], 0), axis=1
    )
    live = jnp.arange(maxb, dtype=jnp.int32)[None, :] < block_counts[:, None]
    mask = jnp.any((block_table[:, :, None] == logical[None, None, :]) & live[:, :, None], axis=1)
    key_row = jnp.arange(width * 2, dtype=jnp.int32) % 2 == 0
    ok = mask[:, None, :, None] & key_row[None, None, None, :]
    ok = jnp.broadcast_to(ok, (ranks, 2, nblk, width * 2)).reshape(group_rows, nblk * width * 2)
    bias = jnp.where(ok, 0.0, NEG).astype(jnp.float32)
    own = jnp.arange(ranks, dtype=jnp.int32) == mine
    parent = fork_parent[0] == mine
    never = jnp.zeros_like(own)
    ex_new = jnp.stack([own, parent], axis=1).reshape(group_rows)
    ex_second = jnp.stack([never, own], axis=1).reshape(group_rows)
    first_row = jnp.arange(width * 2, dtype=jnp.int32) == 0
    exok = jnp.concatenate(
        [ex_new[:, None] & key_row[None], ex_second[:, None] & first_row[None]], axis=1
    )
    exbias = jnp.where(exok, 0.0, NEG).astype(jnp.float32)
    return attend(q, kv, ex, bias, exbias)


def feed(x, norm_gain, w_gate, w_up, w_down):
    scale = lax.rsqrt(jnp.mean(x * x, axis=-1, keepdims=True) + EPS)
    normed = (x * scale * norm_gain.astype(jnp.float32)).astype(jnp.bfloat16)
    rows = normed.shape[0]
    fanout = lax.axis_size("branch")
    ranks = lax.axis_size("attn")
    width = w_gate.shape[1]
    units = w_gate.shape[0]
    columns = lax.all_to_all(
        normed.reshape(rows, fanout, width), "branch", split_axis=1, concat_axis=0, tiled=True
    ).reshape(fanout * rows, width)
    gathered = lax.all_gather(columns, "attn", axis=0, tiled=True)
    ordered = (
        gathered.reshape(ranks, fanout, rows, width)
        .transpose(1, 0, 2, 3)
        .reshape(ranks * fanout * rows, width)
    )
    contract = (((1,), (1,)), ((), ()))
    gate = lax.dot_general(ordered, w_gate, contract, preferred_element_type=jnp.float32)
    upper = lax.dot_general(ordered, w_up, contract, preferred_element_type=jnp.float32)
    both = jnp.concatenate([gate, upper], axis=1).astype(jnp.bfloat16)
    parts = lax.all_to_all(
        both.reshape(fanout, ranks * rows, 2 * units), "branch", split_axis=0, concat_axis=0, tiled=True
    )
    summed = jnp.sum(parts.astype(jnp.float32), axis=0)
    share = (jax.nn.silu(summed[:, :units]) * summed[:, units:]).astype(jnp.bfloat16)
    inner = lax.all_gather(share, "branch", axis=0, tiled=True)
    flipped = (
        inner.reshape(fanout, ranks, rows, units)
        .transpose(1, 0, 2, 3)
        .reshape(ranks * fanout * rows, units)
    )
    down_part = lax.psum_scatter(
        jnp.dot(flipped, w_down, preferred_element_type=jnp.float32),
        "attn",
        scatter_dimension=0,
        tiled=True,
    )
    down = lax.all_to_all(down_part, "branch", split_axis=0, concat_axis=1, tiled=True)
    return (x + down).astype(jnp.bfloat16)


def local(
    queries,
    new_kv,
    tail_kv,
    pool_kv,
    resid,
    block_table,
    block_counts,
    owner_map,
    fork_parent,
    norm_gain,
    w_gate,
    w_up,
    w_down,
):
    ranks = lax.axis_size("attn")
    acc, peak, total = partial_states(
        queries, new_kv, tail_kv, pool_kv, block_table, block_counts, owner_map, fork_parent
    )

    def by_owner(array):
        w = array.shape[2]
        return (
            array.reshape(KVH, GRP, ranks, 2, w).transpose(2, 3, 0, 1, 4).reshape(ranks, 2, H, w)
        )

    packed = jnp.concatenate(
        [by_owner(acc), by_owner(peak[:, :, :1]), by_owner(total[:, :, :1])], axis=3
    ).reshape(ranks, 2 * H * (HD + 2))
    states = lax.all_to_all(packed, "attn", split_axis=0, concat_axis=0, tiled=True)
    states = states.reshape(ranks, 2, H, HD + 2)
    top = jnp.max(states[..., HD], axis=0)
    factor = jnp.exp(states[..., HD] - top)
    summed = jnp.sum(factor * states[..., HD + 1], axis=0)
    mixed = jnp.sum(factor[..., None] * states[..., :HD], axis=0)
    attn = (mixed / summed[..., None]).reshape(2, H * HD).astype(jnp.bfloat16)
    x = resid[:, 0].astype(jnp.float32) + attn.astype(jnp.float32)
    return feed(x, norm_gain, w_gate, w_up, w_down)[:, None]


def solution(mesh):
    return jax.shard_map(
        local,
        mesh=mesh,
        in_specs=(
            P(None, ("branch", "attn"), None),
            P(None, None, ("branch", "attn"), None),
            P(("branch", "attn"), None, None, None),
            P("branch", "attn", None, None, None),
            P(None, ("branch", "attn"), None),
            P("branch", None),
            P("branch"),
            P("branch", None),
            P("branch", None),
            P(),
            P("attn", "branch"),
            P("attn", "branch"),
            P("attn", "branch"),
        ),
        out_specs=P(None, ("branch", "attn"), None),
        check_vma=False,
    )
```

profile of v0, /device:TPU:0, one launch (start us, length us, event | category | flops | bytes accessed | tf_op | source)
XLA Modules:
  0.0 190.1 jit_solution(9958648717776322891)
XLA Ops:
  6.6 0.7 compare_bitcast_fusion
  7.2 0.1 copy.156
  7.3 0.1 copy.133
  7.4 0.1 and.85
  7.5 0.1 stack.10.clone
  7.6 0.1 and.89
  7.7 0.7 iota_compare_fusion.1
  8.4 0.7 reduce.2
  9.1 0.2 select_reduce_fusion
  9.3 1.5 and_reduce_fusion
  10.8 0.1 copy.132
  10.9 0.1 and_select_fusion
  11.0 0.1 copy.162
  11.1 0.7 slice_bitcast_fusion.1
  11.8 1.3 pad_maximum_fusion.2
  13.1 0.1 reshape.213
  13.2 14.7 %reshape_squeeze.3.kv_ref = bf16[4608,1024]{1,0:T(8,128)(2,1)} reshape(bf16[1,36,64,2,1024]{4,3,2,1,0:T(2,128)(2,1)} %param.16) | data formatting | bytes 18874368 | tf_op jit(solution)/shard_map/reshape;squeeze | solution.py:78
  27.9 16.0 %all-gather = bf16[16,1,5120]{2,1,0:T(2,128)(2,1)S(1)} all-gather(bf16[2,1,5120]{2,1,0:T(2,128)(2,1)S(1)} %copy.130), channel_id=2, replica_groups=mesh['branch'=4,'attn'=8] {'attn'}, dimensions={0}, use_global_device_ids=true | all-gather | bytes 184320 | tf_op jit(solution)/shard_map/all_gather | solution.py:72
  43.9 0.9 reduce.1
  44.9 0.2 reshape.211
  45.1 0.1 copy.131
  45.2 0.1 broadcast_and_fusion
  45.4 12.3 %shard_map.127 = (f32[8,80,128]{2,1,0:T(8,128)S(1)}, f32[8,80,128]{2,1,0:T(8,128)S(1)}, f32[8,80,128]{2,1,0:T(8,128)S(1)}) custom-call(bf16[8,80,128]{2,1,0:T(8,128)(2,1)S(1)} %bitcast.81, bf16[4608,1024]{1,0:T(8,128)(2,1)} %reshape_squeeze.3.kv_ref, bf16[256,1024]{1,0:T(8,128)(2,1)S(1)} %fusion.11.ex_ref, f32[16,4608]{1,0:T(8,128)S(1)} %bitcast.80, ...), custom_call_target="tpu_custom_call" | custom-call | tf_op jit(solution)/shard_map/pallas_call | solution.py:47
  57.7 0.6 copy.136
  58.2 0.1 copy.151
  58.3 0.1 reshape.235
  58.5 0.6 copy.138
  59.0 0.1 copy.152
  59.1 0.1 reshape.236
  59.3 0.2 pad_maximum_fusion.1
  59.5 0.2 copy.142
  59.7 1.6 all_to_all.44
  61.3 4.7 %all-to-all-start = ((f32[8,1,10400]{2,1,0:T(1,128)}), f32[8,1,10400]{2,1,0:T(1,128)S(1)}, u32[]{:S(2)}, u32[]{:S(2)}) async-start(f32[8,1,10400]{2,1,0:T(1,128)} %all_to_all.44), calls=%async_computation | async-start | bytes 671744 | tf_op jit(solution)/shard_map/all_to_all | solution.py:179
  66.1 11.2 %all-to-all-done = f32[8,1,10400]{2,1,0:T(1,128)S(1)} async-done(((f32[8,1,10400]{2,1,0:T(1,128)}), f32[8,1,10400]{2,1,0:T(1,128)S(1)}, u32[]{:S(2)}, u32[]{:S(2)}) %all-to-all-start) | async-done | bytes 332832 | tf_op jit(solution)/shard_map/all_to_all | solution.py:179
  77.3 0.8 reduce.3
  78.1 0.8 reshape.220
  78.9 0.2 fusion.20
  79.1 0.2 copy.155
  79.3 0.2 copy.146
  79.5 0.1 fusion.12
  79.7 0.1 fusion.26
  79.8 0.1 fusion.16
  79.8 0.2 fusion.15
  80.0 0.1 multiply_convert_fusion
  80.1 8.2 %all_to_all.49 = bf16[2,4,1280]{2,0,1:T(2,128)(2,1)S(1)} all-to-all(bf16[2,4,1280]{2,0,1:T(2,128)(2,1)S(1)} %copy.147), channel_id=1, replica_groups=mesh['branch'=4,'attn'=8] {'branch'}, dimensions={1} | all-to-all | bytes 40960 | tf_op jit(solution)/shard_map/all_to_all | solution.py:116
  88.4 14.2 %all_gather.10 = bf16[64,1280]{1,0:T(8,128)(2,1)S(1)} all-gather(bf16[8,1280]{1,0:T(8,128)(2,1)S(1)} %reshape.221), channel_id=1, replica_groups=mesh['branch'=4,'attn'=8] {'attn'}, dimensions={0}, use_global_device_ids=true | all-gather | bytes 184320 | tf_op jit(solution)/shard_map/all_gather | solution.py:119
  102.6 0.1 reshape.222
  102.7 0.1 copy.148
  102.8 0.1 dot_general.11
  102.9 5.7 %fusion.4 = bf16[4,16,3072]{2,1,0:T(8,128)(2,1)S(1)} fusion(bf16[4,16,1280]{2,1,0:T(8,128)(2,1)S(1)} %dot_general.11, bf16[3072,1280]{1,0:T(8,128)(2,1)} %param.23), kind=kOutput, calls=%fused_computation.4 | convolution fusion | flops 503513088 | bytes 8421376 | tf_op jit(solution)/shard_map/dot_general | solution.py:126
  108.6 5.7 %fusion.7 = bf16[4,16,3072]{2,1,0:T(8,128)(2,1)S(1)} fusion(bf16[4,16,1280]{2,1,0:T(8,128)(2,1)S(1)} %dot_general.11, bf16[3072,1280]{1,0:T(8,128)(2,1)} %param.24), kind=kOutput, calls=%fused_computation.5 | convolution fusion | flops 503513088 | bytes 8421376 | tf_op jit(solution)/shard_map/dot_general | solution.py:127
  114.3 14.5 %all_to_all.50 = bf16[4,16,6144]{2,1,0:T(8,128)(2,1)S(1)} all-to-all(bf16[4,16,6144]{2,1,0:T(8,128)(2,1)S(1)} %pad_maximum_fusion), channel_id=1, replica_groups=mesh['branch'=4,'attn'=8] {'branch'}, dimensions={0} | all-to-all | bytes 1572864 | tf_op jit(solution)/shard_map/all_to_all | solution.py:129
  128.9 0.1 convert_reduce_fusion
  129.0 0.1 fusion.13
  129.0 9.2 %all_gather.11 = bf16[64,3072]{1,0:T(8,128)(2,1)S(1)} all-gather(bf16[16,3072]{1,0:T(8,128)(2,1)S(1)} %fusion.13), channel_id=1, replica_groups=mesh['branch'=4,'attn'=8] {'branch'}, dimensions={0}, use_global_device_ids=true | all-gather | bytes 491520 | tf_op jit(solution)/shard_map/all_gather | solution.py:134
  138.2 0.1 reshape.223
  138.4 0.3 copy.149
  138.6 0.1 reshape.224
  138.8 5.4 %fusion.21 = f32[64,1280]{1,0:T(8,128)} fusion(bf16[64,3072]{1,0:T(8,128)(2,1)S(1)} %reshape.224, bf16[3072,1280]{1,0:T(8,128)(2,1)} %param.25), kind=kOutput, calls=%fused_computation.49 | convolution fusion | flops 503316480 | bytes 8585216 | tf_op jit(solution)/shard_map/dot_general | solution.py:141
  144.2 28.6 %reduce-scatter.2.cloned.1.call-done = f32[8,1280]{1,0:T(8,128)} async-done(((f32[64,1280]{1,0:T(8,128)}), f32[8,1280]{1,0:T(8,128)}) %reduce-scatter.2.cloned.1.call-update) | async-done | bytes 40976 | tf_op jit(solution)/shard_map/reduce_scatter | solution.py:140
  172.8 1.4 all_to_all.40
  174.2 3.7 %all-to-all-start.3 = ((f32[4,2,1280]{2,1,0:T(2,128)}), f32[4,2,1280]{2,1,0:T(2,128)S(1)}, u32[]{:S(2)}, u32[]{:S(2)}) async-start(f32[4,2,1280]{2,1,0:T(2,128)} %all_to_all.40), calls=%async_computation.4 | async-start | bytes 81920 | tf_op jit(solution)/shard_map/all_to_all | solution.py:146
  177.9 4.8 %all-to-all-done.3 = f32[4,2,1280]{2,1,0:T(2,128)S(1)} async-done(((f32[4,2,1280]{2,1,0:T(2,128)}), f32[4,2,1280]{2,1,0:T(2,128)S(1)}, u32[]{:S(2)}, u32[]{:S(2)}) %all-to-all-start.3) | async-done | bytes 40992 | tf_op jit(solution)/shard_map/all_to_all | solution.py:146
  182.7 0.6 add_convert_fusion
  (29 shorter events, 0.5 us)
Async XLA Ops:
  13.2 14.7 %copy-start.1 = (bf16[2,1,5120]{2,0,1:T(2,128)(2,1)S(1)}, bf16[2,1,5120]{2,0,1:T(2,128)(2,1)}, u32[]{:S(2)}) copy-start(bf16[2,1,5120]{2,0,1:T(2,128)(2,1)} %param.13) | copy-start | bytes 61444
  45.4 20.7 %copy-start = (bf16[2,1,5120]{2,0,1:T(2,128)(2,1)S(1)}, bf16[2,1,5120]{2,0,1:T(2,128)(2,1)}, u32[]{:S(2)}) copy-start(bf16[2,1,5120]{2,0,1:T(2,128)(2,1)} %param.17) | copy-start | bytes 61444
  45.4 20.7 %copy-start.2 = (bf16[5120]{0:T(1024)(128)(2,1)S(1)}, bf16[5120]{0:T(1024)(128)(2,1)}, u32[]{:S(2)}) copy-start(bf16[5120]{0:T(1024)(128)(2,1)} %param.22) | copy-start | bytes 30724
  61.3 16.0 %all-to-all-start = ((f32[8,1,10400]{2,1,0:T(1,128)}), f32[8,1,10400]{2,1,0:T(1,128)S(1)}, u32[]{:S(2)}, u32[]{:S(2)}) async-start(f32[8,1,10400]{2,1,0:T(1,128)} %all_to_all.44), calls=%async_computation | async-start | bytes 671744 | tf_op jit(solution)/shard_map/all_to_all | solution.py:179
  66.0 106.8 %reduce-scatter.2.cloned.1.call-start = ((), (), s32[]{:S(2)}) async-start(), calls=%async_computation.5 | async-start | bytes 368640 | tf_op jit(solution)/shard_map/reduce_scatter | solution.py:140
  174.2 8.4 %all-to-all-start.3 = ((f32[4,2,1280]{2,1,0:T(2,128)}), f32[4,2,1280]{2,1,0:T(2,128)S(1)}, u32[]{:S(2)}, u32[]{:S(2)}) async-start(f32[4,2,1280]{2,1,0:T(2,128)} %all_to_all.40), calls=%async_computation.4 | async-start | bytes 81920 | tf_op jit(solution)/shard_map/all_to_all | solution.py:146
Sparse Core Ops, SparseCore 0:
  144.3 28.4 reduce-scatter.1
where the time goes:
time: 191 us; the launch traced here: 190 us
  blocking collectives  62.1 us (33%)
  waiting for transfers between devices  44.6 us (23%)
  local copies, waits for them, and re-layouts  23.4 us (12%)
  matrix products  16.8 us (9%)
  between operations  13.7 us (7%)
  Pallas kernels  12.3 us (6%)
  other arithmetic  8.85 us (5%)
  starting transfers between devices  8.4 us (4%)
    reduce_scatter x1, waiting for transfers between devices, feed(): lax.psum_scatter(jnp.dot(flipped, w_down, preferred_element_type=jnp.floa...  28.6 us
    all_gather x1, blocking collectives, partial_states(): every_q = lax.all_gather(queries[:, 0], 'attn', axis=0)  16 us
    another operation x1, local copies, waits for them, and re-layouts, partial_states(): kv = pool_kv[0].reshape(nblk * width * 2, kvd)  14.7 us
    all_to_all x1, blocking collectives, feed(): lax.all_to_all(both.reshape(fanout, ranks * rows, 2 * units), 'branch', s...  14.5 us
    all_gather x1, blocking collectives, feed(): gathered = lax.all_gather(columns, 'attn', axis=0, tiled=True)  14.2 us
    pallas_call x1, Pallas kernels, attend(): pl.pallas_call(attend_kernel, grid=(KVH,), in_specs=[head, pl.BlockSpec((...  12.3 us
    all_to_all x1, waiting for transfers between devices, local(): lax.all_to_all(packed, 'attn', split_axis=0, concat_axis=0, tiled=True)  11.2 us
    all_gather x1, blocking collectives, feed(): inner = lax.all_gather(share, 'branch', axis=0, tiled=True)  9.15 us
  transfers between devices with their start and end apart: 3, of which 3 were waited for; matrix products, arithmetic and copies ran while one was open for 0% of the time, Pallas kernels for 0%

commit v1 on v0

--- a/solution.py
+++ b/solution.py
@@ -1,3 +1,5 @@
+import functools
+
 import jax
 import jax.numpy as jnp
 from jax import lax
@@ -105,46 +107,202 @@
     return attend(q, kv, ex, bias, exbias)
 
 
+CHUNKS = 3
+
+
+def feed_kernel(
+    fanout, ranks, rows, nrm_ref, wg_hbm, wu_hbm, wd_hbm, out_ref,
+    wg, wu, wd, cols, gath, xa, xb, part, precv, hid, acc, dperm, dsend, drecv, fsend, frecv,
+    w_sem, a_send, a_recv, b_send, b_recv, p_send, p_recv, h_send, h_recv,
+    d_send, d_recv, f_send, f_recv,
+):
+    me_b = lax.axis_index("branch")
+    me_a = lax.axis_index("attn")
+    uc = wg.shape[1]
+    tokens = xa.shape[0]
+    mesh_id = pl.DeviceIdType.MESH
+
+    loads = []
+    for c in range(CHUNKS):
+        span = pl.ds(c * uc, uc)
+        for k, (src, dst) in enumerate(((wg_hbm, wg), (wu_hbm, wu), (wd_hbm, wd))):
+            loads.append((k, c, pltpu.make_async_copy(src.at[span], dst.at[c], w_sem.at[k, c])))
+    loads.sort(key=lambda item: (item[0] == 2, item[1], item[0]))
+    for _, _, load in loads:
+        load.start()
+    loads = {(k, c): load for k, c, load in loads}
+
+    def at_branch(k):
+        return (lax.rem(me_b + k, fanout), me_a)
+
+    def at_attn(k):
+        return (me_b, lax.rem(me_a + k, ranks))
+
+    barrier = pltpu.get_barrier_semaphore()
+    for k in range(1, fanout):
+        pl.semaphore_signal(barrier, inc=1, device_id=at_branch(k), device_id_type=mesh_id)
+    for k in range(1, ranks):
+        pl.semaphore_signal(barrier, inc=1, device_id=at_attn(k), device_id_type=mesh_id)
+    pl.semaphore_wait(barrier, fanout + ranks - 2)
+
+    def send(src, dst, out_sem, in_sem, where):
+        copy = pltpu.make_async_remote_copy(
+            src_ref=src, dst_ref=dst, send_sem=out_sem, recv_sem=in_sem,
+            device_id=where, device_id_type=mesh_id,
+        )
+        copy.start()
+        return copy
+
+    def finish(copies):
+        for copy in copies:
+            copy.wait_recv()
+
+    sent = []
+    stage = []
+    for k in range(1, fanout):
+        to = lax.rem(me_b + k, fanout)
+        stage.append(send(nrm_ref.at[to], cols.at[me_b], a_send.at[k], a_recv.at[k], at_branch(k)))
+    cols[me_b] = nrm_ref[me_b]
+    finish(stage)
+    sent += stage
+    stage = []
+    for k in range(1, ranks):
+        stage.append(send(cols, gath.at[me_a], b_send.at[k], b_recv.at[k], at_attn(k)))
+    gath[me_a] = cols[...]
+    finish(stage)
+    sent += stage
+    for f in range(fanout):
+        for a in range(ranks):
+            at = (f * ranks + a) * rows
+            xa[at : at + rows, :] = gath[a, f].astype(jnp.float32)
+    xb[...] = xa[...].astype(jnp.bfloat16)
+
+    contract = (((1,), (1,)), ((), ()))
+    parts = []
+    for c in range(CHUNKS):
+        for k, weight in ((0, wg), (1, wu)):
+            loads[k, c].wait()
+            prod = lax.dot_general(
+                xb[...], weight[c], contract, preferred_element_type=jnp.float32
+            ).astype(jnp.bfloat16)
+            part[c, :, :, k * uc : (k + 1) * uc] = prod.reshape(fanout, tokens // fanout, uc)
+        stage = []
+        for k in range(1, fanout):
+            to = lax.rem(me_b + k, fanout)
+            stage.append(
+                send(part.at[c, to], precv.at[c, me_b], p_send.at[c, k], p_recv.at[c, k], at_branch(k))
+            )
+        parts.append(stage)
+        sent += stage
+
+    hidden = []
+    for c in range(CHUNKS):
+        finish(parts[c])
+        summed = part[c, me_b].astype(jnp.float32)
+        for k in range(1, fanout):
+            summed += precv[c, lax.rem(me_b + k, fanout)].astype(jnp.float32)
+        gate = summed[:, :uc]
+        share = gate / (1.0 + jnp.exp(-gate)) * summed[:, uc:]
+        hid[c, me_b] = share.astype(jnp.bfloat16)
+        stage = []
+        for k in range(1, fanout):
+            stage.append(
+                send(hid.at[c, me_b], hid.at[c, me_b], h_send.at[c, k], h_recv.at[c, k], at_branch(k))
+            )
+        hidden.append(stage)
+        sent += stage
+
+    for c in range(CHUNKS):
+        loads[2, c].wait()
+        finish(hidden[c])
+        prod = jnp.dot(
+            hid[c].reshape(tokens, uc), wd[c], preferred_element_type=jnp.float32
+        )
+        acc[...] = prod if c == 0 else acc[...] + prod
+
+    for f in range(fanout):
+        for a in range(ranks):
+            at = (f * ranks + a) * rows
+            dperm[a, f * rows : (f + 1) * rows, :] = acc[at : at + rows, :]
+    dsend[...] = dperm[...].astype(jnp.bfloat16)
+    stage = []
+    for k in range(1, ranks):
+        to = lax.rem(me_a + k, ranks)
+        stage.append(send(dsend.at[to], drecv.at[me_a], d_send.at[k], d_recv.at[k], at_attn(k)))
+    total = dperm[me_a]
+    finish(stage)
+    sent += stage
+    for k in range(1, ranks):
+        total += drecv[lax.rem(me_a + k, ranks)].astype(jnp.float32)
+    for f in range(fanout):
+        fsend[f] = total[f * rows : (f + 1) * rows, :]
+    stage = []
+    for k in range(1, fanout):
+        to = lax.rem(me_b + k, fanout)
+        stage.append(send(fsend.at[to], frecv.at[me_b], f_send.at[k], f_recv.at[k], at_branch(k)))
+    frecv[me_b] = fsend[me_b]
+    finish(stage)
+    out_ref[...] = frecv[...]
+    sent += stage
+    for copy in sent:
+        copy.wait_send()
+
+
 def feed(x, norm_gain, w_gate, w_up, w_down):
     scale = lax.rsqrt(jnp.mean(x * x, axis=-1, keepdims=True) + EPS)
     normed = (x * scale * norm_gain.astype(jnp.float32)).astype(jnp.bfloat16)
     rows = normed.shape[0]
     fanout = lax.axis_size("branch")
     ranks = lax.axis_size("attn")
-    width = w_gate.shape[1]
-    units = w_gate.shape[0]
-    columns = lax.all_to_all(
-        normed.reshape(rows, fanout, width), "branch", split_axis=1, concat_axis=0, tiled=True
-    ).reshape(fanout * rows, width)
-    gathered = lax.all_gather(columns, "attn", axis=0, tiled=True)
-    ordered = (
-        gathered.reshape(ranks, fanout, rows, width)
-        .transpose(1, 0, 2, 3)
-        .reshape(ranks * fanout * rows, width)
-    )
-    contract = (((1,), (1,)), ((), ()))
-    gate = lax.dot_general(ordered, w_gate, contract, preferred_element_type=jnp.float32)
-    upper = lax.dot_general(ordered, w_up, contract, preferred_element_type=jnp.float32)
-    both = jnp.concatenate([gate, upper], axis=1).astype(jnp.bfloat16)
-    parts = lax.all_to_all(
-        both.reshape(fanout, ranks * rows, 2 * units), "branch", split_axis=0, concat_axis=0, tiled=True
-    )
-    summed = jnp.sum(parts.astype(jnp.float32), axis=0)
-    share = (jax.nn.silu(summed[:, :units]) * summed[:, units:]).astype(jnp.bfloat16)
-    inner = lax.all_gather(share, "branch", axis=0, tiled=True)
-    flipped = (
-        inner.reshape(fanout, ranks, rows, units)
-        .transpose(1, 0, 2, 3)
-        .reshape(ranks * fanout * rows, units)
-    )
-    down_part = lax.psum_scatter(
-        jnp.dot(flipped, w_down, preferred_element_type=jnp.float32),
-        "attn",
-        scatter_dimension=0,
-        tiled=True,
-    )
-    down = lax.all_to_all(down_part, "branch", split_axis=0, concat_axis=1, tiled=True)
-    return (x + down).astype(jnp.bfloat16)
+    units, width = w_gate.shape
+    uc = units // CHUNKS
+    tokens = fanout * ranks * rows
+    sliced = normed.reshape(rows, fanout, width).transpose(1, 0, 2)
+    vmem = pl.BlockSpec(memory_space=pltpu.VMEM)
+    hbm = pl.BlockSpec(memory_space=pl.ANY)
+    bf, f32 = jnp.bfloat16, jnp.float32
+    dma = pltpu.SemaphoreType.DMA
+    down = pl.pallas_call(
+        functools.partial(feed_kernel, fanout, ranks, rows),
+        in_specs=[vmem, hbm, hbm, hbm],
+        out_specs=vmem,
+        out_shape=jax.ShapeDtypeStruct((fanout, rows, width), f32),
+        scratch_shapes=[
+            pltpu.VMEM((CHUNKS, uc, width), bf),
+            pltpu.VMEM((CHUNKS, uc, width), bf),
+            pltpu.VMEM((CHUNKS, uc, width), bf),
+            pltpu.VMEM((fanout, rows, width), bf),
+            pltpu.VMEM((ranks, fanout, rows, width), bf),
+            pltpu.VMEM((tokens, width), f32),
+            pltpu.VMEM((tokens, width), bf),
+            pltpu.VMEM((CHUNKS, fanout, tokens // fanout, 2 * uc), bf),
+            pltpu.VMEM((CHUNKS, fanout, tokens // fanout, 2 * uc), bf),
+            pltpu.VMEM((CHUNKS, fanout, tokens // fanout, uc), bf),
+            pltpu.VMEM((tokens, width), f32),
+            pltpu.VMEM((ranks, fanout * rows, width), f32),
+            pltpu.VMEM((ranks, fanout * rows, width), bf),
+            pltpu.VMEM((ranks, fanout * rows, width), bf),
+            pltpu.VMEM((fanout, rows, width), f32),
+            pltpu.VMEM((fanout, rows, width), f32),
+            dma((3, CHUNKS)),
+            dma((fanout,)),
+            dma((fanout,)),
+            dma((ranks,)),
+            dma((ranks,)),
+            dma((CHUNKS, fanout)),
+            dma((CHUNKS, fanout)),
+            dma((CHUNKS, fanout)),
+            dma((CHUNKS, fanout)),
+            dma((ranks,)),
+            dma((ranks,)),
+            dma((fanout,)),
+            dma((fanout,)),
+        ],
+        compiler_params=pltpu.CompilerParams(
+            collective_id=0, has_side_effects=True, vmem_limit_bytes=56 * 1024 * 1024
+        ),
+    )(sliced, w_gate, w_up, w_down)
+    return (x + down.transpose(1, 0, 2).reshape(x.shape)).astype(jnp.bfloat16)
 
 
 def local(

time: 191 us -> 114 us (0.60)
  blocking collectives: 62.1 us -> 16 us
  Pallas kernels: 12.3 us -> 49.6 us
  waiting for transfers between devices: 44.6 us -> 11.3 us
  matrix products: 16.8 us -> 0 us
  between operations: 13.7 us -> 0.26 us
  starting transfers between devices: 8.4 us -> 4.7 us
  local copies, waits for them, and re-layouts: 23.4 us -> 21.1 us
    pallas_call x0 -> x1, Pallas kernels: none -> 37.3 us  [feed(): pl.pallas_call(functools.partial(feed_kernel, fanout, ranks, rows), in_sp...]
    reduce_scatter x1 -> x0, waiting for transfers between devices: 28.6 us -> none  [feed(): lax.psum_scatter(jnp.dot(flipped, w_down, preferred_element_type=jnp.floa...]
    all_gather x2 -> x0, blocking collectives: 23.4 us -> none  [the longest x1 14.2 us: feed(): gathered = lax.all_gather(columns, 'attn', axis=0, tiled=True)]
    all_to_all x2 -> x0, blocking collectives: 22.8 us -> none  [the longest x1 14.5 us: feed(): lax.all_to_all(both.reshape(fanout, ranks * rows, 2 * units), 'branch', s...]
    dot_general x3 -> x0, matrix products: 16.8 us -> none  [the longest x1 5.7 us: feed(): lax.dot_general(ordered, w_gate, contract, preferred_element_type=jnp.flo...]
    all_to_all x1 -> x0, waiting for transfers between devices: 4.75 us -> none  [feed(): lax.all_to_all(down_part, 'branch', split_axis=0, concat_axis=1, tiled=True)]
    all_to_all x1 -> x0, starting transfers between devices: 3.66 us -> none  [feed(): lax.all_to_all(down_part, 'branch', split_axis=0, concat_axis=1, tiled=True)]
  transfers between devices with their start and end apart: 3 -> 1, of which waited for: 3 -> 1; matrix products, arithmetic and copies ran while one was open for 0% -> 0% of each run, Pallas kernels for 0% -> 0%
where the time goes in v1:
time: 114 us; the launch traced here: 113 us
  Pallas kernels  49.6 us (44%)
  local copies, waits for them, and re-layouts  21.1 us (19%)
  blocking collectives  16 us (14%)
  waiting for transfers between devices  11.3 us (10%)
  other arithmetic  10 us (9%)
  starting transfers between devices  4.7 us (4%)
    pallas_call x1, Pallas kernels, feed(): pl.pallas_call(functools.partial(feed_kernel, fanout, ranks, rows), in_sp...  37.3 us
    all_gather x1, blocking collectives, partial_states(): every_q = lax.all_gather(queries[:, 0], 'attn', axis=0)  16 us
    another operation x1, local copies, waits for them, and re-layouts, partial_states(): kv = pool_kv[0].reshape(nblk * width * 2, kvd)  14.7 us
    pallas_call x1, Pallas kernels, attend(): pl.pallas_call(attend_kernel, grid=(KVH,), in_specs=[head, pl.BlockSpec((...  12.3 us
    all_to_all x1, waiting for transfers between devices, local(): lax.all_to_all(packed, 'attn', split_axis=0, concat_axis=0, tiled=True)  11.3 us
    all_to_all x1, starting transfers between devices, local(): lax.all_to_all(packed, 'attn', split_axis=0, concat_axis=0, tiled=True)  4.7 us
  transfers between devices with their start and end apart: 1, of which 1 were waited for; matrix products, arithmetic and copies ran while one was open for 0% of the time, Pallas kernels for 0%

profile of v1, /device:TPU:0, one launch (start us, length us, event | category | flops | bytes accessed | tf_op | source)
XLA Modules:
  0.0 113.0 jit_solution(11043636181173018096)
XLA Ops:
  0.0 0.7 compare_bitcast_fusion
  0.7 0.1 copy.135
  0.8 0.1 copy.115
  0.9 0.1 and.85
  1.0 0.1 stack.10.clone
  1.1 0.1 and.89
  1.2 0.7 iota_compare_fusion.1
  1.9 0.7 reduce.2
  2.6 0.2 select_reduce_fusion
  2.8 1.5 %and_reduce_fusion = pred[8,36]{0,1:T(8,128)(4,1)S(1)} fusion(s32[8,144]{1,0:T(8,128)} %param.18, s32[36]{0:T(128)S(1)} %select_reduce_fusion, pred[8,144]{1,0:T(8,128)(4,1)S(1)} %iota_compare_fusion.1), kind=kLoop, calls=%fused_computation.7 | loop fusion | flops 124128 | bytes 6192 | tf_op jit(solution)/shard_map/reduce_or | solution.py:92
  4.2 0.1 copy.114
  4.3 0.1 and_select_fusion
  4.5 0.1 copy.150
  4.5 0.7 slice_bitcast_fusion.1
  5.3 1.3 %pad_maximum_fusion.1 = bf16[64,2,1024]{2,1,0:T(2,128)(2,1)S(1)} fusion(bf16[1,2,1024]{2,1,0:T(2,128)(2,1)S(1)} %get-tuple-element.14, bf16[63,2,1024]{2,1,0:T(2,128)(2,1)} %bitcast.69), kind=kLoop, calls=%fused_computation.8 | loop fusion | flops 131072 | bytes 524288 | tf_op jit(solution)/shard_map/concatenate | solution.py:81
  6.6 0.1 reshape.192
  6.7 0.0 copy-start.1
  6.7 14.7 %reshape_squeeze.3.kv_ref = bf16[4608,1024]{1,0:T(8,128)(2,1)} reshape(bf16[1,36,64,2,1024]{4,3,2,1,0:T(2,128)(2,1)} %param.16) | data formatting | bytes 18874368 | tf_op jit(solution)/shard_map/reshape;squeeze | solution.py:80
  21.3 0.0 copy-done.1
  21.4 16.0 %all-gather = bf16[16,1,5120]{2,1,0:T(2,128)(2,1)S(1)} all-gather(bf16[2,1,5120]{2,1,0:T(2,128)(2,1)S(1)} %copy.112), channel_id=2, replica_groups=mesh['branch'=4,'attn'=8] {'attn'}, dimensions={0}, use_global_device_ids=true | all-gather | bytes 184320 | tf_op jit(solution)/shard_map/all_gather | solution.py:74
  37.4 0.9 reduce.1
  38.3 0.2 reshape.190
  38.6 0.1 copy.113
  38.7 0.1 broadcast_and_fusion
  38.8 0.0 copy-start.2
  38.8 12.3 %shard_map.127 = (f32[8,80,128]{2,1,0:T(8,128)S(1)}, f32[8,80,128]{2,1,0:T(8,128)S(1)}, f32[8,80,128]{2,1,0:T(8,128)S(1)}) custom-call(bf16[8,80,128]{2,1,0:T(8,128)(2,1)S(1)} %bitcast.62, bf16[4608,1024]{1,0:T(8,128)(2,1)} %reshape_squeeze.3.kv_ref, bf16[256,1024]{1,0:T(8,128)(2,1)S(1)} %fusion.1.ex_ref, f32[16,4608]{1,0:T(8,128)S(1)} %bitcast.61, ...), custom_call_target="tpu_custom_call" | custom-call | tf_op jit(solution)/shard_map/pallas_call | solution.py:49
  51.1 0.0 copy-start
  51.2 0.6 copy.118
  51.7 0.1 copy.130
  51.8 0.1 reshape.209
  52.0 0.6 copy.120
  52.5 0.1 copy.131
  52.6 0.1 reshape.210
  52.8 0.2 pad_maximum_fusion
  52.9 0.2 copy.124
  53.2 1.6 %all_to_all.8 = f32[8,1,10400]{2,1,0:T(1,128)} reshape(f32[8,2,40,130]{3,2,1,0:T(8,128)S(1)} %copy.124) | data formatting | bytes 665600 | tf_op jit(solution)/shard_map/all_to_all | solution.py:337
  54.8 4.7 %all-to-all-start = ((f32[8,1,10400]{2,1,0:T(1,128)}), f32[8,1,10400]{2,1,0:T(1,128)S(1)}, u32[]{:S(2)}, u32[]{:S(2)}) async-start(f32[8,1,10400]{2,1,0:T(1,128)} %all_to_all.8), calls=%async_computation | async-start | bytes 671744 | tf_op jit(solution)/shard_map/all_to_all | solution.py:337
  59.5 0.0 copy-done.2
  59.5 11.3 %all-to-all-done = f32[8,1,10400]{2,1,0:T(1,128)S(1)} async-done(((f32[8,1,10400]{2,1,0:T(1,128)}), f32[8,1,10400]{2,1,0:T(1,128)S(1)}, u32[]{:S(2)}, u32[]{:S(2)}) %all-to-all-start) | async-done | bytes 332832 | tf_op jit(solution)/shard_map/all_to_all | solution.py:337
  70.8 0.8 reduce.3
  71.6 0.8 reshape.199
  72.4 0.2 fusion.13
  72.6 0.2 copy.134
  72.7 0.2 copy.128
  73.0 0.1 fusion.2
  73.1 0.1 fusion.8
  73.2 0.1 fusion.14
  73.4 0.0 copy-done
  73.4 0.2 fusion.4
  73.6 0.7 fusion.9.nrm_ref
  74.3 37.3 %shard_map.128 = f32[4,2,1280]{2,1,0:T(2,128)} custom-call(bf16[4,2,1280]{2,1,0:T(2,128)(2,1)} %fusion.9.nrm_ref, bf16[3072,1280]{1,0:T(8,128)(2,1)} %wg_hbm.1, bf16[3072,1280]{1,0:T(8,128)(2,1)} %wu_hbm.1, bf16[3072,1280]{1,0:T(8,128)(2,1)} %wd_hbm.1), custom_call_target="tpu_custom_call" | custom-call | tf_op jit(solution)/shard_map/pallas_call | solution.py:265
  111.6 1.4 %add_convert_fusion = bf16[2,1,5120]{2,0,1:T(2,128)(2,1)} fusion(f32[2,1,5120]{2,0,1:T(2,128)} %bitcast.71, f32[2,1,5120]{2,0,1:T(2,128)S(1)} %reshape.201, bf16[2,1,5120]{2,0,1:T(2,128)(2,1)S(1)} %copy-done), kind=kLoop, calls=%fused_computation.17 | loop fusion | flops 40960 | bytes 122880 | tf_op jit(solution)/shard_map/convert_element_type | solution.py:305
  (17 shorter events, 0.3 us)
Async XLA Ops:
  6.7 14.7 %copy-start.1 = (bf16[2,1,5120]{2,0,1:T(2,128)(2,1)S(1)}, bf16[2,1,5120]{2,0,1:T(2,128)(2,1)}, u32[]{:S(2)}) copy-start(bf16[2,1,5120]{2,0,1:T(2,128)(2,1)} %param.13) | copy-start | bytes 61444
  38.8 20.6 %copy-start.2 = (bf16[5120]{0:T(1024)(128)(2,1)S(1)}, bf16[5120]{0:T(1024)(128)(2,1)}, u32[]{:S(2)}) copy-start(bf16[5120]{0:T(1024)(128)(2,1)} %param.22) | copy-start | bytes 30724
  51.1 22.2 %copy-start = (bf16[2,1,5120]{2,0,1:T(2,128)(2,1)S(1)}, bf16[2,1,5120]{2,0,1:T(2,128)(2,1)}, u32[]{:S(2)}) copy-start(bf16[2,1,5120]{2,0,1:T(2,128)(2,1)} %param.17) | copy-start | bytes 61444
  54.8 16.0 %all-to-all-start = ((f32[8,1,10400]{2,1,0:T(1,128)}), f32[8,1,10400]{2,1,0:T(1,128)S(1)}, u32[]{:S(2)}, u32[]{:S(2)}) async-start(f32[8,1,10400]{2,1,0:T(1,128)} %all_to_all.8), calls=%async_computation | async-start | bytes 671744 | tf_op jit(solution)/shard_map/all_to_all | solution.py:337

commit v2 on v1

--- a/solution.py
+++ b/solution.py
@@ -71,7 +71,7 @@
     maxb = block_table.shape[1]
     pool_size = owner_map.shape[1]
     group_rows = 2 * ranks
-    every_q = lax.all_gather(queries[:, 0], "attn", axis=0)
+    (every_q,) = swap([queries[:, 0]], True, 1)
     q = (
         every_q.reshape(group_rows, KVH, GRP, HD)
         .transpose(1, 2, 0, 3)
@@ -105,6 +105,58 @@
     )
     exbias = jnp.where(exok, 0.0, NEG).astype(jnp.float32)
     return attend(q, kv, ex, bias, exbias)
+
+
+def swap_kernel(ranks, gathers, *refs):
+    count = (len(refs) - 2) // 3
+    ins, outs, bufs = refs[:count], refs[count : 2 * count], refs[2 * count : 3 * count]
+    out_sem, in_sem = refs[3 * count :]
+    me_b = lax.axis_index("branch")
+    me = lax.axis_index("attn")
+    mesh_id = pl.DeviceIdType.MESH
+    barrier = pltpu.get_barrier_semaphore()
+    for k in range(1, ranks):
+        pl.semaphore_signal(
+            barrier, inc=1, device_id=(me_b, lax.rem(me + k, ranks)), device_id_type=mesh_id
+        )
+    pl.semaphore_wait(barrier, ranks - 1)
+    copies = []
+    for k in range(1, ranks):
+        to = lax.rem(me + k, ranks)
+        for i in range(count):
+            copy = pltpu.make_async_remote_copy(
+                src_ref=ins[i] if gathers else ins[i].at[to],
+                dst_ref=bufs[i].at[me],
+                send_sem=out_sem.at[i, k],
+                recv_sem=in_sem.at[i, k],
+                device_id=(me_b, to),
+                device_id_type=mesh_id,
+            )
+            copy.start()
+            copies.append(copy)
+    for i in range(count):
+        bufs[i][me] = ins[i][...] if gathers else ins[i][me]
+    for copy in copies:
+        copy.wait_recv()
+    for i in range(count):
+        outs[i][...] = bufs[i][...]
+    for copy in copies:
+        copy.wait_send()
+
+
+def swap(arrays, gathers, collective_id):
+    ranks = lax.axis_size("attn")
+    shapes = [((ranks,) + a.shape if gathers else a.shape, a.dtype) for a in arrays]
+    vmem = pl.BlockSpec(memory_space=pltpu.VMEM)
+    return pl.pallas_call(
+        functools.partial(swap_kernel, ranks, gathers),
+        in_specs=[vmem] * len(arrays),
+        out_specs=[vmem] * len(arrays),
+        out_shape=[jax.ShapeDtypeStruct(*shape) for shape in shapes],
+        scratch_shapes=[pltpu.VMEM(*shape) for shape in shapes]
+        + [pltpu.SemaphoreType.DMA((len(arrays), ranks))] * 2,
+        compiler_params=pltpu.CompilerParams(collective_id=collective_id, has_side_effects=True),
+    )(*arrays)
 
 
 CHUNKS = 3
@@ -328,18 +380,15 @@
     def by_owner(array):
         w = array.shape[2]
         return (
-            array.reshape(KVH, GRP, ranks, 2, w).transpose(2, 3, 0, 1, 4).reshape(ranks, 2, H, w)
+            array.reshape(KVH, GRP, ranks, 2, w).transpose(2, 3, 0, 1, 4).reshape(ranks, 2 * H, w)
         )
 
-    packed = jnp.concatenate(
-        [by_owner(acc), by_owner(peak[:, :, :1]), by_owner(total[:, :, :1])], axis=3
-    ).reshape(ranks, 2 * H * (HD + 2))
-    states = lax.all_to_all(packed, "attn", split_axis=0, concat_axis=0, tiled=True)
-    states = states.reshape(ranks, 2, H, HD + 2)
-    top = jnp.max(states[..., HD], axis=0)
-    factor = jnp.exp(states[..., HD] - top)
-    summed = jnp.sum(factor * states[..., HD + 1], axis=0)
-    mixed = jnp.sum(factor[..., None] * states[..., :HD], axis=0)
+    stats = jnp.stack([by_owner(peak[:, :, :1])[..., 0], by_owner(total[:, :, :1])[..., 0]], axis=1)
+    accs, stats = swap([by_owner(acc), stats], False, 2)
+    top = jnp.max(stats[:, 0], axis=0)
+    factor = jnp.exp(stats[:, 0] - top)
+    summed = jnp.sum(factor * stats[:, 1], axis=0)
+    mixed = jnp.sum(factor[..., None] * accs, axis=0)
     attn = (mixed / summed[..., None]).reshape(2, H * HD).astype(jnp.bfloat16)
     x = resid[:, 0].astype(jnp.float32) + attn.astype(jnp.float32)
     return feed(x, norm_gain, w_gate, w_up, w_down)[:, None]

time: 114 us -> 107 us (0.939)
  Pallas kernels: 49.6 us -> 74.9 us
  blocking collectives: 16 us -> 0 us
  waiting for transfers between devices: 11.3 us -> 0 us
  starting transfers between devices: 4.7 us -> 0 us
    pallas_call x0 -> x2, Pallas kernels: none -> 21.8 us  [swap(): pl.pallas_call(functools.partial(swap_kernel, ranks, gathers), in_specs=[...]
    all_gather x1 -> x0, blocking collectives: 16 us -> none  [partial_states(): every_q = lax.all_gather(queries[:, 0], 'attn', axis=0)]
    all_to_all x1 -> x0, waiting for transfers between devices: 11.3 us -> none  [local(): lax.all_to_all(packed, 'attn', split_axis=0, concat_axis=0, tiled=True)]
    all_to_all x1 -> x0, starting transfers between devices: 4.7 us -> none  [local(): lax.all_to_all(packed, 'attn', split_axis=0, concat_axis=0, tiled=True)]
    pallas_call x1, Pallas kernels: 37.3 us -> 40.7 us  [feed(): pl.pallas_call(functools.partial(feed_kernel, fanout, ranks, rows), in_sp...]
    all_to_all x1 -> x0, local copies, waits for them, and re-layouts: 1.61 us -> none  [local(): lax.all_to_all(packed, 'attn', split_axis=0, concat_axis=0, tiled=True)]
  transfers between devices with their start and end apart: 1 -> 0, of which waited for: 1 -> 0; matrix products, arithmetic and copies ran while one was open for 0% -> 0% of each run, Pallas kernels for 0% -> 0%
where the time goes in v2:
time: 107 us; the launch traced here: 106 us
  Pallas kernels  74.9 us (70%)
  local copies, waits for them, and re-layouts  21.5 us (20%)
  other arithmetic  9.4 us (9%)
    pallas_call x1, Pallas kernels, feed(): pl.pallas_call(functools.partial(feed_kernel, fanout, ranks, rows), in_sp...  40.7 us
    pallas_call x2, Pallas kernels, swap(): pl.pallas_call(functools.partial(swap_kernel, ranks, gathers), in_specs=[...  21.8 us
    another operation x1, local copies, waits for them, and re-layouts, partial_states(): kv = pool_kv[0].reshape(nblk * width * 2, kvd)  14.7 us
    pallas_call x1, Pallas kernels, attend(): pl.pallas_call(attend_kernel, grid=(KVH,), in_specs=[head, pl.BlockSpec((...  12.3 us

profile of v2, /device:TPU:0, one launch (start us, length us, event | category | flops | bytes accessed | tf_op | source)
XLA Modules:
  0.0 105.9 jit_solution(14791594862114818984)
XLA Ops:
  0.0 0.7 compare_bitcast_fusion
  0.7 0.1 copy.52
  0.8 0.1 and.85
  0.9 0.1 copy.64
  1.0 0.1 stack.13.clone
  1.0 0.1 and.89
  1.2 0.1 broadcast_and_fusion
  1.2 0.7 reduce.1
  1.9 0.2 select_reduce_fusion
  2.1 0.7 iota_compare_fusion.1
  2.9 1.5 %and_reduce_fusion = pred[8,36]{0,1:T(8,128)(4,1)S(1)} fusion(s32[8,144]{1,0:T(8,128)} %param.18, s32[36]{0:T(128)S(1)} %select_reduce_fusion, pred[8,144]{1,0:T(8,128)(4,1)S(1)} %iota_compare_fusion.1), kind=kLoop, calls=%fused_computation.5 | loop fusion | flops 124128 | bytes 6192 | tf_op jit(solution)/shard_map/reduce_or | solution.py:92
  4.3 0.1 copy.51
  4.4 0.1 and_select_fusion
  4.6 0.1 copy.78
  4.6 0.7 slice_bitcast_fusion.1
  5.3 1.3 %pad_maximum_fusion = bf16[64,2,1024]{2,1,0:T(2,128)(2,1)S(1)} fusion(bf16[1,2,1024]{2,1,0:T(2,128)(2,1)S(1)} %get-tuple-element.17, bf16[63,2,1024]{2,1,0:T(2,128)(2,1)} %bitcast.72), kind=kLoop, calls=%fused_computation.6 | loop fusion | flops 131072 | bytes 524288 | tf_op jit(solution)/shard_map/concatenate | solution.py:81
  6.6 0.1 reshape.184
  6.8 14.7 %reshape_squeeze.3.kv_ref = bf16[4608,1024]{1,0:T(8,128)(2,1)} reshape(bf16[1,36,64,2,1024]{4,3,2,1,0:T(2,128)(2,1)} %param.16) | data formatting | bytes 18874368 | tf_op jit(solution)/shard_map/reshape;squeeze | solution.py:80
  21.5 0.0 copy-start
  21.5 0.0 copy-start.1
  21.5 10.3 %shard_map.127 = bf16[8,2,5120]{2,1,0:T(2,128)(2,1)} custom-call(bf16[2,5120]{1,0:T(2,128)(2,1)} %bitcast.77), custom_call_target="tpu_custom_call" | custom-call | tf_op jit(solution)/shard_map/pallas_call | solution.py:151
  31.8 1.1 %reshape.182 = bf16[16,8,5,128]{3,2,1,0:T(8,128)(2,1)S(1)} reshape(bf16[8,2,5120]{2,1,0:T(2,128)(2,1)} %shard_map.127) | data formatting | bytes 327680 | tf_op jit(solution)/shard_map/reshape | solution.py:76
  32.9 0.1 copy.50
  33.0 12.3 %shard_map.128 = (f32[8,80,128]{2,1,0:T(8,128)S(1)}, f32[8,80,128]{2,1,0:T(8,128)S(1)}, f32[8,80,128]{2,1,0:T(8,128)S(1)}) custom-call(bf16[8,80,128]{2,1,0:T(8,128)(2,1)S(1)} %bitcast.65, bf16[4608,1024]{1,0:T(8,128)(2,1)} %reshape_squeeze.3.kv_ref, bf16[256,1024]{1,0:T(8,128)(2,1)S(1)} %fusion.1.ex_ref, f32[16,4608]{1,0:T(8,128)S(1)} %bitcast.64, ...), custom_call_target="tpu_custom_call" | custom-call | tf_op jit(solution)/shard_map/pallas_call | solution.py:49
  45.3 0.6 copy.55
  45.8 0.2 copy.56
  46.0 0.1 stack_squeeze_reshape.6
  46.1 0.6 copy.57
  46.6 0.2 copy.58
  46.8 0.1 stack_squeeze_reshape.7
  46.9 0.6 pad_maximum_fusion.1.refs_1_
  47.6 0.8 copy.61.refs_0_
  48.3 11.5 %shard_map.129 = (f32[8,80,128]{2,1,0:T(8,128)}, f32[8,2,80]{2,1,0:T(2,128)}) custom-call(f32[8,80,128]{2,1,0:T(8,128)} %copy.61.refs_0_, f32[8,2,80]{2,1,0:T(2,128)} %pad_maximum_fusion.1.refs_1_), custom_call_target="tpu_custom_call" | custom-call | tf_op jit(solution)/shard_map/pallas_call | solution.py:151
  59.9 0.7 copy.62
  60.6 0.7 slice.24
  61.3 0.1 div.32
  61.4 0.1 div.33
  61.5 1.1 %multiply_reduce_fusion = f32[80,128]{1,0:T(8,128)S(1)} fusion(f32[8,80,128]{2,1,0:T(8,128)} %get-tuple-element.14, f32[8,80]{1,0:T(8,128)S(1)} %get-tuple-element.16), kind=kLoop, calls=%fused_computation.3 | loop fusion | flops 153600 | bytes 371200 | tf_op jit(solution)/shard_map/reduce_sum | solution.py:391
  62.7 0.1 broadcast_bitcast_fusion
  62.8 0.0 copy-done
  62.8 0.2 fusion.3
  63.0 0.0 copy-done.1
  63.0 0.7 fusion.5.nrm_ref
  63.7 40.7 %shard_map.130 = f32[4,2,1280]{2,1,0:T(2,128)} custom-call(bf16[4,2,1280]{2,1,0:T(2,128)(2,1)} %fusion.5.nrm_ref, bf16[3072,1280]{1,0:T(8,128)(2,1)} %wg_hbm.1, bf16[3072,1280]{1,0:T(8,128)(2,1)} %wu_hbm.1, bf16[3072,1280]{1,0:T(8,128)(2,1)} %wd_hbm.1), custom_call_target="tpu_custom_call" | custom-call | tf_op jit(solution)/shard_map/pallas_call | solution.py:317
  104.5 1.4 %add_convert_fusion = bf16[2,1,5120]{2,0,1:T(2,128)(2,1)} fusion(f32[2,1,5120]{2,0,1:T(2,128)} %bitcast.74, f32[2,1,5120]{2,0,1:T(2,128)S(1)} %reduce_sum.44, f32[2,1,5120]{2,0,1:T(2,128)S(1)} %div.34, bf16[2,1,5120]{2,0,1:T(2,128)(2,1)S(1)} %copy-done), kind=kLoop, calls=%fused_computation.14 | loop fusion | flops 71680 | bytes 163840 | tf_op jit(solution)/shard_map/convert_element_type | solution.py:357
  (19 shorter events, 0.3 us)
Async XLA Ops:
  21.5 41.3 %copy-start = (bf16[2,1,5120]{2,0,1:T(2,128)(2,1)S(1)}, bf16[2,1,5120]{2,0,1:T(2,128)(2,1)}, u32[]{:S(2)}) copy-start(bf16[2,1,5120]{2,0,1:T(2,128)(2,1)} %param.17) | copy-start | bytes 61444
  21.5 41.5 %copy-start.1 = (bf16[5120]{0:T(1024)(128)(2,1)S(1)}, bf16[5120]{0:T(1024)(128)(2,1)}, u32[]{:S(2)}) copy-start(bf16[5120]{0:T(1024)(128)(2,1)} %param.22) | copy-start | bytes 30724

commit v3 on v2

--- a/solution.py
+++ b/solution.py
@@ -71,7 +71,12 @@
     maxb = block_table.shape[1]
     pool_size = owner_map.shape[1]
     group_rows = 2 * ranks
-    (every_q,) = swap([queries[:, 0]], True, 1)
+    pieces = [queries[:, 0]] + [
+        lax.ppermute(queries[:, 0], "attn", [(a, (a + k) % ranks) for a in range(ranks)])
+        for k in range(1, ranks)
+    ]
+    backward = jnp.stack((pieces[::-1]) * 2)
+    every_q = lax.dynamic_slice_in_dim(backward, ranks - 1 - mine, ranks, 0)
     q = (
         every_q.reshape(group_rows, KVH, GRP, HD)
         .transpose(1, 2, 0, 3)

time: 107 us -> 108 us (level)
  Pallas kernels: 74.9 us -> 62.6 us
  starting transfers between devices: 0 us -> 9.38 us
  waiting for transfers between devices: 0 us -> 4.09 us
    pallas_call x2 -> x1, Pallas kernels: 21.8 us -> 11 us  [swap(): pl.pallas_call(functools.partial(swap_kernel, ranks, gathers), in_specs=[...]
    ppermute x0 -> x7, starting transfers between devices: none -> 9.38 us  [partial_states(): lax.ppermute(queries[:, 0], 'attn', [(a, (a + k) % ranks) for a in range(...]
    ppermute x0 -> x7, waiting for transfers between devices: none -> 4.09 us  [partial_states(): lax.ppermute(queries[:, 0], 'attn', [(a, (a + k) % ranks) for a in range(...]
    pallas_call x1, Pallas kernels: 40.7 us -> 39.4 us  [feed(): pl.pallas_call(functools.partial(feed_kernel, fanout, ranks, rows), in_sp...]
  transfers between devices with their start and end apart: 0 -> 7, of which waited for: 0 -> 2; matrix products, arithmetic and copies ran while one was open for 0% -> 20% of each run, Pallas kernels for 0% -> 0%
where the time goes in v3:
time: 108 us; the launch traced here: 107 us
  Pallas kernels  62.6 us (58%)
  local copies, waits for them, and re-layouts  21.1 us (20%)
  other arithmetic  9.39 us (9%)
  starting transfers between devices  9.38 us (9%)
  waiting for transfers between devices  4.09 us (4%)
    pallas_call x1, Pallas kernels, feed(): pl.pallas_call(functools.partial(feed_kernel, fanout, ranks, rows), in_sp...  39.4 us
    another operation x1, local copies, waits for them, and re-layouts, partial_states(): kv = pool_kv[0].reshape(nblk * width * 2, kvd)  14.7 us
    pallas_call x1, Pallas kernels, attend(): pl.pallas_call(attend_kernel, grid=(KVH,), in_specs=[head, pl.BlockSpec((...  12.3 us
    pallas_call x1, Pallas kernels, swap(): pl.pallas_call(functools.partial(swap_kernel, ranks, gathers), in_specs=[...  11 us
    ppermute x7, starting transfers between devices, partial_states(): lax.ppermute(queries[:, 0], 'attn', [(a, (a + k) % ranks) for a in range(...  9.38 us
    ppermute x7, waiting for transfers between devices, partial_states(): lax.ppermute(queries[:, 0], 'attn', [(a, (a + k) % ranks) for a in range(...  4.09 us
  transfers between devices with their start and end apart: 7, of which 2 were waited for; matrix products, arithmetic and copies ran while one was open for 20% of the time, Pallas kernels for 0%

profile of v3, /device:TPU:0, one launch (start us, length us, event | category | flops | bytes accessed | tf_op | source)
XLA Modules:
  0.0 106.9 jit_solution(8461536021010894104)
XLA Ops:
  0.0 4.5 %collective-permute-start = (bf16[2,5120]{1,0:T(2,128)(2,1)}, bf16[2,5120]{1,0:T(2,128)(2,1)S(1)}, u32[]{:S(2)}, u32[]{:S(2)}) collective-permute-start(bf16[2,5120]{1,0:T(2,128)(2,1)} %bitcast.101), channel_id=1, source_target_pairs={{0,7},{1,0},{2,1},{3,2},{4,3},{5,4},{6,5},{7,6},{8,15},{9,8},{10,9... | collective-permute-start | bytes 61448 | tf_op jit(solution)/shard_map/ppermute | solution.py:75
  4.5 0.6 collective-permute-start.1
  5.1 0.0 collective-permute-start.2
  5.1 2.8 %collective-permute-start.3 = (bf16[2,5120]{1,0:T(2,128)(2,1)}, bf16[2,5120]{1,0:T(2,128)(2,1)S(1)}, u32[]{:S(2)}, u32[]{:S(2)}) collective-permute-start(bf16[2,5120]{1,0:T(2,128)(2,1)} %bitcast.104), channel_id=1, source_target_pairs={{0,4},{1,5},{2,6},{3,7},{4,0},{5,1},{6,2},{7,3},{8,12},{9,13},{10,... | collective-permute-start | bytes 61448 | tf_op jit(solution)/shard_map/ppermute | solution.py:75
  7.8 0.0 collective-permute-start.4
  7.8 0.7 compare_bitcast_fusion
  8.5 0.1 copy.63
  8.6 0.1 copy.51
  8.7 0.1 and.85
  8.8 0.1 stack.52.clone
  8.9 0.1 and.89
  9.0 0.7 iota_compare_fusion.1
  9.7 0.7 reduce.1
  10.4 0.2 select_reduce_fusion
  10.6 1.5 %and_reduce_fusion = pred[8,36]{0,1:T(8,128)(4,1)S(1)} fusion(s32[8,144]{1,0:T(8,128)} %param.18, s32[36]{0:T(128)S(1)} %select_reduce_fusion, pred[8,144]{1,0:T(8,128)(4,1)S(1)} %iota_compare_fusion.1), kind=kLoop, calls=%fused_computation.5 | loop fusion | flops 124128 | bytes 6192 | tf_op jit(solution)/shard_map/reduce_or | solution.py:97
  12.1 0.1 copy.50
  12.1 0.7 slice_bitcast_fusion.1
  12.9 1.3 %pad_maximum_fusion = bf16[64,2,1024]{2,1,0:T(2,128)(2,1)S(1)} fusion(bf16[1,2,1024]{2,1,0:T(2,128)(2,1)S(1)} %get-tuple-element.17, bf16[63,2,1024]{2,1,0:T(2,128)(2,1)} %bitcast.96), kind=kLoop, calls=%fused_computation.6 | loop fusion | flops 131072 | bytes 524288 | tf_op jit(solution)/shard_map/concatenate | solution.py:86
  14.2 0.1 reshape.184
  14.3 0.1 and_select_fusion
  14.4 0.1 broadcast_and_fusion
  14.5 0.1 copy.77
  14.6 0.0 copy-start.2
  14.6 0.0 copy-start.1
  14.6 14.7 %reshape_squeeze.3.kv_ref = bf16[4608,1024]{1,0:T(8,128)(2,1)} reshape(bf16[1,36,64,2,1024]{4,3,2,1,0:T(2,128)(2,1)} %param.16) | data formatting | bytes 18874368 | tf_op jit(solution)/shard_map/reshape;squeeze | solution.py:85
  29.3 0.0 copy-done.2
  29.3 0.0 collective-permute-done
  29.3 0.0 copy-done.1
  29.3 0.7 collective-permute-start.5
  30.0 0.0 collective-permute-done.1
  30.0 0.9 collective-permute-start.6
  31.0 0.0 collective-permute-done.2
  31.0 0.0 collective-permute-done.3
  31.0 0.0 collective-permute-done.4
  31.1 4.0 %collective-permute-done.5 = bf16[2,5120]{1,0:T(2,128)(2,1)S(1)} collective-permute-done((bf16[2,5120]{1,0:T(2,128)(2,1)S(1)}, bf16[2,5120]{1,0:T(2,128)(2,1)S(1)}, u32[]{:S(2)}, u32[]{:S(2)}) %collective-permute-start.5) | collective-permute-done | bytes 20512 | tf_op jit(solution)/shard_map/ppermute | solution.py:75
  35.1 0.0 copy-start
  35.1 0.1 collective-permute-done.6
  35.5 0.1 constant_dynamic-slice_fusion
  35.6 0.2 reshape.182
  35.8 0.1 copy.49
  35.9 12.3 %shard_map.127 = (f32[8,80,128]{2,1,0:T(8,128)S(1)}, f32[8,80,128]{2,1,0:T(8,128)S(1)}, f32[8,80,128]{2,1,0:T(8,128)S(1)}) custom-call(bf16[8,80,128]{2,1,0:T(8,128)(2,1)S(1)} %bitcast.89, bf16[4608,1024]{1,0:T(8,128)(2,1)} %reshape_squeeze.3.kv_ref, bf16[256,1024]{1,0:T(8,128)(2,1)S(1)} %fusion.1.ex_ref, f32[16,4608]{1,0:T(8,128)S(1)} %bitcast.88, ...), custom_call_target="tpu_custom_call" | custom-call | tf_op jit(solution)/shard_map/pallas_call | solution.py:49
  48.2 0.6 copy.54
  48.7 0.2 copy.55
  48.9 0.1 stack_squeeze_reshape.6
  49.0 0.6 copy.56
  49.5 0.2 copy.57
  49.7 0.1 stack_squeeze_reshape.7
  49.8 0.8 copy.60.refs_0_
  50.6 0.6 pad_maximum_fusion.1.refs_1_
  51.2 11.0 %shard_map.128 = (f32[8,80,128]{2,1,0:T(8,128)}, f32[8,2,80]{2,1,0:T(2,128)}) custom-call(f32[8,80,128]{2,1,0:T(8,128)} %copy.60.refs_0_, f32[8,2,80]{2,1,0:T(2,128)} %pad_maximum_fusion.1.refs_1_), custom_call_target="tpu_custom_call" | custom-call | tf_op jit(solution)/shard_map/pallas_call | solution.py:156
  62.2 0.7 copy.61
  62.9 0.7 slice.24
  63.6 1.1 %multiply_reduce_fusion = f32[80,128]{1,0:T(8,128)S(1)} fusion(f32[8,80,128]{2,1,0:T(8,128)} %get-tuple-element.14, f32[8,80]{1,0:T(8,128)S(1)} %get-tuple-element.16), kind=kLoop, calls=%fused_computation.3 | loop fusion | flops 153600 | bytes 371200 | tf_op jit(solution)/shard_map/reduce_sum | solution.py:396
  64.8 0.1 div.32
  64.9 0.1 broadcast_bitcast_fusion
  65.0 0.1 div.33
  65.2 0.0 copy-done
  65.2 0.2 fusion.3
  65.4 0.7 fusion.5.nrm_ref
  66.1 39.4 %shard_map.129 = f32[4,2,1280]{2,1,0:T(2,128)} custom-call(bf16[4,2,1280]{2,1,0:T(2,128)(2,1)} %fusion.5.nrm_ref, bf16[3072,1280]{1,0:T(8,128)(2,1)} %wg_hbm.1, bf16[3072,1280]{1,0:T(8,128)(2,1)} %wu_hbm.1, bf16[3072,1280]{1,0:T(8,128)(2,1)} %wd_hbm.1), custom_call_target="tpu_custom_call" | custom-call | tf_op jit(solution)/shard_map/pallas_call | solution.py:322
  105.4 1.4 %add_convert_fusion = bf16[2,1,5120]{2,0,1:T(2,128)(2,1)} fusion(f32[2,1,5120]{2,0,1:T(2,128)} %bitcast.98, f32[2,1,5120]{2,0,1:T(2,128)S(1)} %reduce_sum.44, f32[2,1,5120]{2,0,1:T(2,128)S(1)} %div.34, bf16[2,1,5120]{2,0,1:T(2,128)(2,1)S(1)} %copy-done), kind=kLoop, calls=%fused_computation.14 | loop fusion | flops 71680 | bytes 163840 | tf_op jit(solution)/shard_map/convert_element_type | solution.py:362
  (35 shorter events, 0.7 us)
Async XLA Ops:
  0.0 29.3 %collective-permute-start = (bf16[2,5120]{1,0:T(2,128)(2,1)}, bf16[2,5120]{1,0:T(2,128)(2,1)S(1)}, u32[]{:S(2)}, u32[]{:S(2)}) collective-permute-start(bf16[2,5120]{1,0:T(2,128)(2,1)} %bitcast.101), channel_id=1, source_target_pairs={{0,7},{1,0},{2,1},{3,2},{4,3},{5,4},{6,5},{7,6},{8,15},{9,8},{10,9... | collective-permute-start | bytes 61448 | tf_op jit(solution)/shard_map/ppermute | solution.py:75
  4.5 25.5 %collective-permute-start.1 = (bf16[2,5120]{1,0:T(2,128)(2,1)}, bf16[2,5120]{1,0:T(2,128)(2,1)S(1)}, u32[]{:S(2)}, u32[]{:S(2)}) collective-permute-start(bf16[2,5120]{1,0:T(2,128)(2,1)} %bitcast.102), channel_id=1, source_target_pairs={{0,6},{1,7},{2,0},{3,1},{4,2},{5,3},{6,4},{7,5},{8,14},{9,15},{10,... | collective-permute-start | bytes 61448 | tf_op jit(solution)/shard_map/ppermute | solution.py:75
  5.1 25.9 %collective-permute-start.2 = (bf16[2,5120]{1,0:T(2,128)(2,1)}, bf16[2,5120]{1,0:T(2,128)(2,1)S(1)}, u32[]{:S(2)}, u32[]{:S(2)}) collective-permute-start(bf16[2,5120]{1,0:T(2,128)(2,1)} %bitcast.103), channel_id=1, source_target_pairs={{0,5},{1,6},{2,7},{3,0},{4,1},{5,2},{6,3},{7,4},{8,13},{9,14},{10,... | collective-permute-start | bytes 61448 | tf_op jit(solution)/shard_map/ppermute | solution.py:75
  5.1 25.9 %collective-permute-start.3 = (bf16[2,5120]{1,0:T(2,128)(2,1)}, bf16[2,5120]{1,0:T(2,128)(2,1)S(1)}, u32[]{:S(2)}, u32[]{:S(2)}) collective-permute-start(bf16[2,5120]{1,0:T(2,128)(2,1)} %bitcast.104), channel_id=1, source_target_pairs={{0,4},{1,5},{2,6},{3,7},{4,0},{5,1},{6,2},{7,3},{8,12},{9,13},{10,... | collective-permute-start | bytes 61448 | tf_op jit(solution)/shard_map/ppermute | solution.py:75
  7.8 23.2 %collective-permute-start.4 = (bf16[2,5120]{1,0:T(2,128)(2,1)}, bf16[2,5120]{1,0:T(2,128)(2,1)S(1)}, u32[]{:S(2)}, u32[]{:S(2)}) collective-permute-start(bf16[2,5120]{1,0:T(2,128)(2,1)} %bitcast.105), channel_id=1, source_target_pairs={{0,3},{1,4},{2,5},{3,6},{4,7},{5,0},{6,1},{7,2},{8,11},{9,12},{10,... | collective-permute-start | bytes 61448 | tf_op jit(solution)/shard_map/ppermute | solution.py:75
  14.6 14.7 %copy-start.2 = (bf16[5120]{0:T(1024)(128)(2,1)S(1)}, bf16[5120]{0:T(1024)(128)(2,1)}, u32[]{:S(2)}) copy-start(bf16[5120]{0:T(1024)(128)(2,1)} %param.22) | copy-start | bytes 30724
  14.6 14.7 %copy-start.1 = (bf16[2,1,5120]{2,0,1:T(2,128)(2,1)S(1)}, bf16[2,1,5120]{2,0,1:T(2,128)(2,1)}, u32[]{:S(2)}) copy-start(bf16[2,1,5120]{2,0,1:T(2,128)(2,1)} %param.13) | copy-start | bytes 61444
  29.3 5.7 %collective-permute-start.5 = (bf16[2,5120]{1,0:T(2,128)(2,1)S(1)}, bf16[2,5120]{1,0:T(2,128)(2,1)S(1)}, u32[]{:S(2)}, u32[]{:S(2)}) collective-permute-start(bf16[2,5120]{1,0:T(2,128)(2,1)S(1)} %bitcast.106), channel_id=1, source_target_pairs={{0,2},{1,3},{2,4},{3,5},{4,6},{5,7},{6,0},{7,1},{8,10},{9,11},{10,... | collective-permute-start | bytes 61448 | tf_op jit(solution)/shard_map/ppermute | solution.py:75
  30.0 5.2 %collective-permute-start.6 = (bf16[2,5120]{1,0:T(2,128)(2,1)S(1)}, bf16[2,5120]{1,0:T(2,128)(2,1)S(1)}, u32[]{:S(2)}, u32[]{:S(2)}) collective-permute-start(bf16[2,5120]{1,0:T(2,128)(2,1)S(1)} %bitcast.107), channel_id=1, source_target_pairs={{0,1},{1,2},{2,3},{3,4},{4,5},{5,6},{6,7},{7,0},{8,9},{9,10},{10,1... | collective-permute-start | bytes 61448 | tf_op jit(solution)/shard_map/ppermute | solution.py:75
  35.1 30.1 %copy-start = (bf16[2,1,5120]{2,0,1:T(2,128)(2,1)S(1)}, bf16[2,1,5120]{2,0,1:T(2,128)(2,1)}, u32[]{:S(2)}) copy-start(bf16[2,1,5120]{2,0,1:T(2,128)(2,1)} %param.17) | copy-start | bytes 61444
